TPU v7x, 512 devices: a whole 4x8x8 slice. The times are simulated.
512 devices in a mesh: batch: 32 (over z_lo, y, core), gy: 4 (over z_hi), gx: 4 (over x).
Axes of the slice: x: 4, y: 8, z: 8 (z_hi: 4, z_lo: 2; z = z_hi * 2 + z_lo), core: 2. Of those that a mesh axis runs over, the one named last changes fastest.
Arguments:
- x_fine: bfloat16 [32, 32, 128, 256], P('batch', 'gy', 'gx'), may hold values from -6 to 6
- dy_fine: bfloat16 [32, 32, 128, 256], P('batch', 'gy', 'gx'), may hold values from -6 to 6
- x_coarse: bfloat16 [32, 16, 16, 1024], P('batch', 'gy', 'gx'), may hold values from -6 to 6
- dy_coarse: bfloat16 [32, 16, 16, 1024], P('batch', 'gy', 'gx'), may hold values from -6 to 6
- timestep: int32 [32], P('batch'), may hold values from 0 to 999
- fine_gain: float32 [256], replicated, may hold values from 0.5 to 2.5, as said below
- coarse_gain: float32 [1024], replicated, may hold values from 0.5 to 2.5, as said below
- fine_qkv: bfloat16 [256, 768], replicated, may hold values from -0.375 to 0.375
- fine_out: bfloat16 [256, 256], replicated, may hold values from -0.375 to 0.375
- coarse_qkv: bfloat16 [3, 1024, 1024], P(None, ('gy', 'gx')), may hold values from -0.1875 to 0.1875
- coarse_out: bfloat16 [1024, 1024], P(('gy', 'gx')), may hold values from -0.1875 to 0.1875
Outputs:
- dx_fine: bfloat16 [32, 32, 128, 256], P('batch', 'gy', 'gx')
- dx_coarse: bfloat16 [32, 16, 16, 1024], P('batch', 'gy', 'gx')
- grad_fine_qkv: bfloat16 [256, 768], replicated
- grad_fine_out: bfloat16 [256, 256], replicated
- grad_coarse_qkv: bfloat16 [3, 1024, 1024], P(None, ('gy', 'gx'))
- grad_coarse_out: bfloat16 [1024, 1024], P(('gy', 'gx'))
Inputs may be any that keep to these rules, and one draw needn't show every extreme that they name: `fine_gain`: the norm gains are positive. `coarse_gain`: the norm gains are positive.
All inputs are finite; a program needn't handle non-finite values.
Results may differ from a plain program's by a relative error of at most 0.017.
The roundings to bfloat16 on the way count: a program that leaves them out, or rounds other values in their place, can miss the bound.
Values may be sent and summed in bfloat16 or wider, within the bound.
A program may use at most 64 MiB of HBM per device.

v0:
```python
import math
import jax
import jax.numpy as jnp
from jax import lax
from jax.sharding import PartitionSpec as P

D_F = 256
H_F = 4
D_C = 1024
HD = 64
RAD = 3
eps = 1e-06
log_span = math.log(1000.0)
block_side = 8


def padded_2(array, sides, width):
    for axis, dim in sides:
        peers, length = (lax.axis_size(axis), array.shape[dim])
        up = [(i, (i + 1) % peers) for i in range(peers - 1)]
        down = [(j, i) for i, j in up]
        last = lax.slice_in_dim(array, length - width, length, axis=dim)
        leading = lax.slice_in_dim(array, 0, width, axis=dim)
        before = lax.ppermute(last, axis, up)
        after = lax.ppermute(leading, axis, down)
        array = jnp.concatenate([before, array, after], axis=dim)
    return array


def shifted(value, axis, steps):
    count = lax.axis_size(axis)
    leading, last = (max(0, -steps), min(count, count - steps))
    return lax.ppermute(value, axis, [(source, source + steps) for source in range(leading, last)])


def contract(pattern, first_op, second_op):
    return jnp.einsum(pattern, first_op, second_op, preferred_element_type=jnp.float32)


def score_scale():
    return 1.0 / math.sqrt(HD)


def time_gain(gains, step_value):
    channels = gains.shape[0]
    frequency = jnp.exp(-log_span * jnp.arange(channels, dtype=jnp.float32) / channels)
    return gains * (1.0 + 0.5 * jnp.cos(step_value.astype(jnp.float32) * frequency))


def norm_forward(source, factor):
    floats = source.astype(jnp.float32)
    inverse = lax.rsqrt(jnp.mean(floats * floats, axis=-1, keepdims=True) + eps)
    return ((floats * inverse * factor).astype(jnp.bfloat16), inverse)


def norm_backward(source, inverse, factor, upstream):
    floats = source.astype(jnp.float32)
    scaled = upstream * factor
    middle = jnp.mean(floats * scaled, axis=-1, keepdims=True)
    return (inverse * scaled - floats * inverse * inverse * inverse * middle).astype(jnp.bfloat16)


def to_tiles(planar):
    height, breadth, channels = planar.shape
    pieces = planar.reshape(
        height // block_side, block_side, breadth // block_side, block_side, channels
    )
    return pieces.transpose(0, 2, 1, 3, 4).reshape(-1, block_side * block_side, channels)


def from_tiles(blocks, height, breadth):
    channels = blocks.shape[-1]
    pieces = blocks.reshape(
        height // block_side, breadth // block_side, block_side, block_side, channels
    )
    return pieces.transpose(0, 2, 1, 3, 4).reshape(height, breadth, channels)


def windows(padded, height, breadth):
    extent = block_side + 2 * RAD
    block_rows = height // block_side
    across = breadth // block_side
    channels = padded.shape[-1]
    widened = jnp.pad(
        padded,
        (
            (0, (block_rows + 1) * block_side - padded.shape[0]),
            (0, (across + 1) * block_side - padded.shape[1]),
            (0, 0),
        ),
    )
    blocks_grid = widened.reshape(
        block_rows + 1, block_side, across + 1, block_side, channels
    ).transpose(0, 2, 1, 3, 4)
    upper_pair = jnp.concatenate([blocks_grid[:-1, :-1], blocks_grid[:-1, 1:]], axis=3)
    lower_pair = jnp.concatenate([blocks_grid[1:, :-1], blocks_grid[1:, 1:]], axis=3)
    square = jnp.concatenate([upper_pair, lower_pair], axis=2)
    return square[:, :, :extent, :extent].reshape(block_rows * across, extent * extent, channels)


def intersection_add(windowed, height, breadth):
    extent = block_side + 2 * RAD
    block_rows = height // block_side
    across = breadth // block_side
    channels = windowed.shape[-1]
    layout = windowed.reshape(block_rows, across, extent, extent, channels)
    layout = jnp.pad(
        layout, ((0, 0), (0, 0), (0, 2 * block_side - extent), (0, 2 * block_side - extent), (0, 0))
    )
    summed = jnp.zeros((block_rows + 1, across + 1, block_side, block_side, channels), jnp.float32)
    for row_half in range(2):
        for col_half in range(2):
            quarter = layout[
                :,
                :,
                row_half * block_side : (row_half + 1) * block_side,
                col_half * block_side : (col_half + 1) * block_side,
            ]
            summed = summed + jnp.pad(
                quarter,
                ((row_half, 1 - row_half), (col_half, 1 - col_half), (0, 0), (0, 0), (0, 0)),
            )
    merged = summed.transpose(0, 2, 1, 3, 4).reshape(
        (block_rows + 1) * block_side, (across + 1) * block_side, channels
    )
    return merged[: height + 2 * RAD, : breadth + 2 * RAD]


def pair_mask():
    extent = block_side + 2 * RAD
    inner_pos = jnp.arange(block_side * block_side)
    outer_pos = jnp.arange(extent * extent)
    row_gap = outer_pos[None, :] // extent - inner_pos[:, None] // block_side
    col_gap = outer_pos[None, :] % extent - inner_pos[:, None] % block_side
    return (row_gap >= 0) & (row_gap <= 2 * RAD) & (col_gap >= 0) & (col_gap <= 2 * RAD)


def fine_forward(queries, key_values, valid_pad):
    height, breadth, channels = queries.shape
    query_blocks = to_tiles(queries)
    block_count = query_blocks.shape[0]
    query_heads = query_blocks.reshape(block_count, -1, H_F, HD)
    key_windows = windows(key_values, height, breadth)
    key_heads = key_windows[..., :channels].reshape(block_count, -1, H_F, HD)
    value_heads = key_windows[..., channels:].reshape(block_count, -1, H_F, HD)
    allowed = (
        pair_mask()[None, None]
        & windows(valid_pad[..., None], height, breadth)[:, None, None, :, 0]
    )
    scores = contract("bqhe,bkhe->bhqk", query_heads, key_heads) * score_scale()
    scores = jnp.where(allowed, scores, -1e30)
    peak = jnp.max(scores, axis=-1, keepdims=True)
    log_total = peak + jnp.log(jnp.sum(jnp.exp(scores - peak), axis=-1, keepdims=True))
    shares = jnp.where(allowed, jnp.exp(scores - log_total), 0.0)
    weights = shares.astype(jnp.bfloat16)
    mixed = contract("bhqk,bkhe->bqhe", weights, value_heads).astype(jnp.bfloat16)
    attended = from_tiles(mixed.reshape(block_count, -1, channels), height, breadth)
    return (attended, query_heads, key_heads, value_heads, shares, weights, log_total)


def fine_query_backward(upstream, query_heads, key_heads, value_heads, shares, height, breadth):
    block_count = query_heads.shape[0]
    upward_heads = to_tiles(upstream).reshape(block_count, -1, H_F, HD)
    products = contract("bqhe,bkhe->bhqk", upward_heads, value_heads)
    centre = jnp.sum(shares * products, axis=-1, keepdims=True)
    slopes = (shares * (products - centre)).astype(jnp.bfloat16)
    grad_query = contract("bhqk,bkhe->bqhe", slopes, key_heads) * score_scale()
    grad_query = from_tiles(grad_query.reshape(block_count, -1, H_F * HD), height, breadth)
    return (grad_query, upward_heads, slopes, centre)


def key_grads_windows(slopes, weights, query_heads, upward_heads):
    block_count = query_heads.shape[0]
    grad_key = contract("bhqk,bqhe->bkhe", slopes, query_heads).reshape(block_count, -1, D_F)
    grad_value = contract("bhqk,bqhe->bkhe", weights, upward_heads).reshape(block_count, -1, D_F)
    return jnp.concatenate([grad_key, grad_value], axis=-1)


def local(
    x_fine,
    dy_fine,
    x_coarse,
    dy_coarse,
    timestep,
    fine_gain,
    coarse_gain,
    fine_qkv,
    fine_out,
    coarse_qkv,
    coarse_out,
):
    step_value = timestep[0]
    picture = x_fine[0]
    height, breadth = (picture.shape[0], picture.shape[1])
    factor = time_gain(fine_gain, step_value)
    normed, inverse = norm_forward(picture, factor)
    flat_normed = normed.reshape(-1, D_F)
    projected = (
        jnp.dot(flat_normed, fine_qkv, preferred_element_type=jnp.float32)
        .astype(jnp.bfloat16)
        .reshape(height, breadth, 3 * D_F)
    )
    queries = projected[..., :D_F]
    key_values = projected[..., D_F:]
    kv_pad = padded_2(key_values[None], (("gy", 1), ("gx", 2)), RAD)[0]
    row_first = lax.axis_index("gy") * height - RAD
    col_first = lax.axis_index("gx") * breadth - RAD
    pad_rows = row_first + jnp.arange(height + 2 * RAD, dtype=jnp.int32)
    pad_cols = col_first + jnp.arange(breadth + 2 * RAD, dtype=jnp.int32)
    rows_inside = (pad_rows >= 0) & (pad_rows < height * lax.axis_size("gy"))
    cols_inside = (pad_cols >= 0) & (pad_cols < breadth * lax.axis_size("gx"))
    valid_pad = rows_inside[:, None] & cols_inside[None, :]
    attended, query_heads, key_heads, value_heads, shares, weights, log_total = fine_forward(
        queries, kv_pad, valid_pad
    )
    flat_cot = dy_fine[0].reshape(-1, D_F)
    grad_out_local = lax.dot_general(
        attended.reshape(-1, D_F),
        flat_cot,
        (((0,), (0,)), ((), ())),
        preferred_element_type=jnp.float32,
    )
    upstream = (
        lax.dot_general(
            flat_cot, fine_out, (((1,), (1,)), ((), ())), preferred_element_type=jnp.float32
        )
        .astype(jnp.bfloat16)
        .reshape(height, breadth, D_F)
    )
    grad_query, upward_heads, slopes, centre = fine_query_backward(
        upstream, query_heads, key_heads, value_heads, shares, height, breadth
    )
    summed = intersection_add(
        key_grads_windows(slopes, weights, query_heads, upward_heads), height, breadth
    )
    from_left = shifted(summed[:, breadth + RAD :], "gx", 1)
    from_right = shifted(summed[:, :RAD], "gx", -1)
    middle = summed[:, RAD : breadth + RAD]
    middle = middle.at[:, :RAD].add(from_left)
    middle = middle.at[:, breadth - RAD :].add(from_right)
    from_above = shifted(middle[height + RAD :], "gy", 1)
    from_below = shifted(middle[:RAD], "gy", -1)
    key_grads = middle[RAD : height + RAD]
    key_grads = key_grads.at[:RAD].add(from_above)
    key_grads = key_grads.at[height - RAD :].add(from_below)
    grad_proj = (
        jnp.concatenate(
            [grad_query, key_grads[..., :D_F] * score_scale(), key_grads[..., D_F:]], axis=-1
        )
        .astype(jnp.bfloat16)
        .reshape(-1, 3 * D_F)
    )
    grad_qkv_local = lax.dot_general(
        flat_normed, grad_proj, (((0,), (0,)), ((), ())), preferred_element_type=jnp.float32
    )
    down_grad = lax.dot_general(
        grad_proj, fine_qkv, (((1,), (1,)), ((), ())), preferred_element_type=jnp.float32
    ).reshape(height, breadth, D_F)
    dx_picture = norm_backward(picture, inverse, factor, down_grad)
    coarse_tokens = x_coarse[0].reshape(-1, D_C)
    coarse_factor = time_gain(coarse_gain, step_value)
    coarse_normed, coarse_inverse = norm_forward(coarse_tokens, coarse_factor)
    coarse_cot = dy_coarse[0].reshape(-1, D_C)
    all_normed = lax.all_gather(coarse_normed, ("gy", "gx"), axis=0, tiled=True)
    coarse_proj = contract("td,khd->kth", all_normed, coarse_qkv).astype(jnp.bfloat16)
    head_queries, head_keys, head_values = (coarse_proj[0], coarse_proj[1], coarse_proj[2])
    coarse_scores = contract("te,se->ts", head_queries, head_keys) * score_scale()
    coarse_peak = jnp.max(coarse_scores, axis=-1, keepdims=True)
    coarse_log = coarse_peak + jnp.log(
        jnp.sum(jnp.exp(coarse_scores - coarse_peak), axis=-1, keepdims=True)
    )
    coarse_shares = jnp.exp(coarse_scores - coarse_log)
    coarse_weights = coarse_shares.astype(jnp.bfloat16)
    head_mixed = contract("ts,se->te", coarse_weights, head_values).astype(jnp.bfloat16)
    all_cot = lax.all_gather(coarse_cot, ("gy", "gx"), axis=0, tiled=True)
    head_upstream = contract("td,ed->te", all_cot, coarse_out).astype(jnp.bfloat16)
    coarse_out_local = contract("te,td->ed", head_mixed, all_cot)
    coarse_products = contract("te,se->ts", head_upstream, head_values)
    coarse_centre = jnp.sum(coarse_shares * coarse_products, axis=-1, keepdims=True)
    coarse_slopes = (coarse_shares * (coarse_products - coarse_centre)).astype(jnp.bfloat16)
    head_grad_query = (contract("ts,se->te", coarse_slopes, head_keys) * score_scale()).astype(
        jnp.bfloat16
    )
    head_grad_key = (contract("ts,te->se", coarse_slopes, head_queries) * score_scale()).astype(
        jnp.bfloat16
    )
    head_grad_value = contract("ts,te->se", coarse_weights, head_upstream).astype(jnp.bfloat16)
    stacked = jnp.stack([head_grad_query, head_grad_key, head_grad_value])
    coarse_qkv_local = contract("kte,td->ked", stacked, all_normed)
    head_part = contract("kte,ked->td", stacked, coarse_qkv)
    coarse_down = lax.psum_scatter(
        head_part.astype(jnp.bfloat16), ("gy", "gx"), scatter_dimension=0, tiled=True
    ).astype(jnp.float32)
    dx_coarse_tok = norm_backward(coarse_tokens, coarse_inverse, coarse_factor, coarse_down)
    fine_qkv_sum, fine_out_sum = lax.psum((grad_qkv_local, grad_out_local), ("batch", "gy", "gx"))
    coarse_qkv_sum, coarse_out_sum = lax.psum((coarse_qkv_local, coarse_out_local), "batch")
    return (
        dx_picture[None],
        dx_coarse_tok.reshape(x_coarse.shape),
        fine_qkv_sum.astype(jnp.bfloat16),
        fine_out_sum.astype(jnp.bfloat16),
        coarse_qkv_sum.astype(jnp.bfloat16),
        coarse_out_sum.astype(jnp.bfloat16),
    )


def solution(mesh):
    placed = (
        P("batch", "gy", "gx", None),
        P("batch", "gy", "gx", None),
        P("batch", "gy", "gx", None),
        P("batch", "gy", "gx", None),
        P("batch"),
        P(),
        P(),
        P(),
        P(),
        P(None, ("gy", "gx"), None),
        P(("gy", "gx"), None),
    )
    return jax.shard_map(
        local,
        mesh=mesh,
        in_specs=placed,
        out_specs=(
            P("batch", "gy", "gx", None),
            P("batch", "gy", "gx", None),
            P(),
            P(),
            P(None, ("gy", "gx"), None),
            P(("gy", "gx"), None),
        ),
        check_vma=False,
    )
```

profile of v0, /device:TPU:1, one launch (start us, length us, event | category | flops | bytes accessed | tf_op | source)
XLA Modules:
  0.0 400.2 jit_solution(13088266657257998717)
XLA Ops:
  7.9 1.0 fusion.28
  10.3 1.0 fusion.20
  11.3 1.3 convolution_convert_fusion
  12.7 6.8 %collective-permute-start = (bf16[1,3,32,512]{3,2,1,0:T(8,128)(2,1)S(1)}, bf16[1,3,32,512]{3,2,1,0:T(8,128)(2,1)S(1)}, u32[]{:S(2)}, u32[]{:S(2)}) collective-permute-start(bf16[1,3,32,512]{3,2,1,0:T(8,128)(2,1)S(1)} %get-tuple-element.74), channel_id=1, source_target_pairs={{0,4},{4,8},{8,12},{1,5},{5,9},{9,13},{2,6},{6,10},{10,14},{3,7},{... | collective-permute-start | bytes 294920 | tf_op jit(solution)/shard_map/ppermute | solution.py:24
  19.4 1.3 collective-permute-start.1
  21.1 44.2 %all_gather.6 = bf16[256,1024]{1,0:T(8,128)(2,1)S(1)} all-gather(bf16[16,1024]{1,0:T(8,128)(2,1)S(1)} %multiply_convert_fusion.2), channel_id=1, replica_groups=mesh['batch'=32,'gy'=4,'gx'=4] {'gy','gx'}, dimensions={0}, use_global_device_ids=true | all-gather | bytes 557056 | tf_op jit(solution)/shard_map/all_gather | solution.py:264
  66.0 34.0 %all_gather.7 = bf16[256,1024]{1,0:T(8,128)(2,1)S(1)} all-gather(bf16[16,1024]{1,0:T(8,128)(2,1)S(1)} %reshape_squeeze.8), channel_id=1, replica_groups=mesh['batch'=32,'gy'=4,'gx'=4] {'gy','gx'}, dimensions={0}, use_global_device_ids=true | all-gather | bytes 557056 | tf_op jit(solution)/shard_map/all_gather | solution.py:275
  101.2 1.1 fusion.1
  103.5 131.1 %all-reduce.11 = (bf16[3,64,1024]{2,1,0:T(8,128)(2,1)}, bf16[64,1024]{1,0:T(8,128)(2,1)}) all-reduce(f32[3,64,1024]{2,1,0:T(8,128)S(1)} %fusion.14, f32[64,1024]{1,0:T(8,128)S(1)} %fusion.9), channel_id=1, replica_groups=mesh['batch'=32,'gy'=4,'gx'=4] {'batch'}, use_global_device_ids=true, to_apply=%region_13.14 | all-reduce | flops 262144 | bytes 1572864 | tf_op jit(solution)/shard_map/psum | solution.py:296
  235.0 2.2 collective-permute-start.2
  237.2 1.5 collective-permute-start.3
  239.5 2.6 collective-permute-done.3
  246.8 1.0 fusion.4
  247.8 1.3 convolution_bitcast_fusion.2
  249.5 2.0 copy.49
  251.6 1.9 concatenate.57
  253.5 1.1 copy.51
  254.6 1.9 concatenate.58
  256.7 0.9 copy-done.2
  258.7 1.0 copy.52
  260.5 2.6 collective-permute-start.4
  263.0 0.9 fusion.64
  264.5 1.3 collective-permute-start.5
  265.8 0.9 slice_add_fusion.3
  267.2 2.9 collective-permute-done.5
  270.5 1.4 collective-permute-start.6
  272.0 1.3 collective-permute-start.7
  273.3 1.2 collective-permute-done.6
  274.6 6.9 %collective-permute-done.7 = f32[3,32,512]{2,1,0:T(8,128)S(1)} collective-permute-done((f32[3,32,512]{2,1,0:T(8,128)S(1)}, f32[3,32,512]{2,1,0:T(8,128)S(1)}, u32[]{:S(2)}, u32[]{:S(2)}) %collective-permute-start.7) | collective-permute-done | bytes 196640 | tf_op jit(solution)/shard_map/ppermute | solution.py:33
  283.8 107.2 %all-reduce.12 = (bf16[256,768]{1,0:T(8,128)(2,1)}, bf16[256,256]{1,0:T(8,128)(2,1)}) all-reduce(f32[256,768]{1,0:T(8,128)S(1)} %convolution_bitcast_fusion.3, f32[256,256]{1,0:T(8,128)S(1)} %copy-done.5), channel_id=1, replica_groups=mesh['batch'=32,'gy'=4,'gx'=4] {'batch','gy','gx'}, use_global_device_ids=true, to_apply=%region_11.12 | all-reduce | flops 262144 | bytes 1572864 | tf_op jit(solution)/shard_map/psum | solution.py:295
  391.0 0.9 multiply_reduce_fusion.2
  391.9 0.8 subtract_convert_fusion
  (138 shorter events, 17.1 us)
Async XLA Ops:
  7.2 58.1 %copy-start = (bf16[3,64,1024]{2,1,0:T(8,128)(2,1)S(1)}, bf16[3,64,1024]{2,1,0:T(8,128)(2,1)}, u32[]{:S(2)}) copy-start(bf16[3,64,1024]{2,1,0:T(8,128)(2,1)} %param.28) | copy-start | bytes 1179652
  7.2 13.6 %copy-start.10 = (bf16[1,4,4,1024]{3,2,1,0:T(4,128)(2,1)S(1)}, bf16[1,4,4,1024]{3,2,1,0:T(4,128)(2,1)}, u32[]{:S(2)}) copy-start(bf16[1,4,4,1024]{3,2,1,0:T(4,128)(2,1)} %param.21) | copy-start | bytes 98308
  7.2 13.8 %copy-start.21 = (f32[1024]{0:T(1024)S(1)}, f32[1024]{0:T(1024)}, u32[]{:S(2)}) copy-start(f32[1024]{0:T(1024)} %param.25) | copy-start | bytes 12292
  7.2 13.8 %copy-start.16 = (bf16[1,4,4,1024]{3,2,1,0:T(4,128)(2,1)S(1)}, bf16[1,4,4,1024]{3,2,1,0:T(4,128)(2,1)}, u32[]{:S(2)}) copy-start(bf16[1,4,4,1024]{3,2,1,0:T(4,128)(2,1)} %param.22) | copy-start | bytes 98308
  7.2 383.7 %reduce-scatter.2.cloned.1.call-start = ((), (), s32[]{:S(2)}) async-start(), calls=%async_computation.1 | async-start | bytes 557056 | tf_op jit(solution)/shard_map/reduce_scatter | solution.py:291
  9.0 0.6 copy-start.14
  10.3 55.0 %copy-start.19 = (f32[256]{0:T(256)}, f32[256]{0:T(256)S(1)}, u32[]{:S(2)}) copy-start(f32[256]{0:T(256)S(1)} %add_multiply_fusion.1) | copy-start | bytes 3076
  12.7 87.4 %copy-start.11 = (bf16[64,1024]{1,0:T(8,128)(2,1)S(1)}, bf16[64,1024]{1,0:T(8,128)(2,1)}, u32[]{:S(2)}) copy-start(bf16[64,1024]{1,0:T(8,128)(2,1)} %param.29) | copy-start | bytes 393220
  12.7 222.2 %collective-permute-start = (bf16[1,3,32,512]{3,2,1,0:T(8,128)(2,1)S(1)}, bf16[1,3,32,512]{3,2,1,0:T(8,128)(2,1)S(1)}, u32[]{:S(2)}, u32[]{:S(2)}) collective-permute-start(bf16[1,3,32,512]{3,2,1,0:T(8,128)(2,1)S(1)} %get-tuple-element.74), channel_id=1, source_target_pairs={{0,4},{4,8},{8,12},{1,5},{5,9},{9,13},{2,6},{6,10},{10,14},{3,7},{... | collective-permute-start | bytes 294920 | tf_op jit(solution)/shard_map/ppermute | solution.py:24
  19.4 215.5 %collective-permute-start.1 = (bf16[1,3,32,512]{3,2,1,0:T(8,128)(2,1)S(1)}, bf16[1,3,32,512]{3,2,1,0:T(8,128)(2,1)S(1)}, u32[]{:S(2)}, u32[]{:S(2)}) collective-permute-start(bf16[1,3,32,512]{3,2,1,0:T(8,128)(2,1)S(1)} %get-tuple-element.75), channel_id=1, source_target_pairs={{4,0},{8,4},{12,8},{5,1},{9,5},{13,9},{6,2},{10,6},{14,10},{7,3},{... | collective-permute-start | bytes 294920 | tf_op jit(solution)/shard_map/ppermute | solution.py:25
  21.0 44.3 %copy-start.17 = (f32[16]{0:T(128)}, f32[16]{0:T(128)S(1)}, u32[]{:S(2)}) copy-start(f32[16]{0:T(128)S(1)} %rsqrt.26) | copy-start | bytes 196
  21.0 79.3 %copy-start.12 = (f32[1024]{0:T(1024)}, f32[1024]{0:T(1024)S(1)}, u32[]{:S(2)}) copy-start(f32[1024]{0:T(1024)S(1)} %add_multiply_fusion) | copy-start | bytes 12292
  102.3 1.0 copy-start.6
  102.3 1.0 copy-start.9
  235.0 4.5 %collective-permute-start.2 = (bf16[1,14,3,512]{3,2,1,0:T(4,128)(2,1)S(1)}, bf16[1,14,3,512]{3,2,1,0:T(4,128)(2,1)S(1)}, u32[]{:S(2)}, u32[]{:S(2)}) collective-permute-start(bf16[1,14,3,512]{3,2,1,0:T(4,128)(2,1)S(1)} %get-tuple-element.72), channel_id=1, source_target_pairs={{0,1},{1,2},{2,3},{4,5},{5,6},{6,7},{8,9},{9,10},{10,11},{12,13},{... | collective-permute-start | bytes 129032 | tf_op jit(solution)/shard_map/ppermute | solution.py:24
  237.2 4.9 %collective-permute-start.3 = (bf16[1,14,3,512]{3,2,1,0:T(4,128)(2,1)S(1)}, bf16[1,14,3,512]{3,2,1,0:T(4,128)(2,1)S(1)}, u32[]{:S(2)}, u32[]{:S(2)}) collective-permute-start(bf16[1,14,3,512]{3,2,1,0:T(4,128)(2,1)S(1)} %get-tuple-element.73), channel_id=1, source_target_pairs={{1,0},{2,1},{3,2},{5,4},{6,5},{7,6},{9,8},{10,9},{11,10},{13,12},{... | collective-permute-start | bytes 129032 | tf_op jit(solution)/shard_map/ppermute | solution.py:25
  254.5 1.9 copy-start.1
  256.5 1.1 copy-start.2
  258.7 4.3 %copy-start.7 = (bf16[1,8,32,256]{3,2,1,0:T(8,128)(2,1)S(1)}, bf16[1,8,32,256]{3,2,1,0:T(8,128)(2,1)}, u32[]{:S(2)}) copy-start(bf16[1,8,32,256]{3,2,1,0:T(8,128)(2,1)} %param.20) | copy-start | bytes 393220
  259.8 4.3 %copy-start.4 = (bf16[4,64,4,64]{1,3,2,0:T(8,128)(2,1)S(1)}, bf16[4,64,4,64]{1,3,2,0:T(8,128)(2,1)}, u32[]{:S(2)}) copy-start(bf16[4,64,4,64]{1,3,2,0:T(8,128)(2,1)} %fusion.4) | copy-start | bytes 393220
  260.5 5.4 %collective-permute-start.4 = (f32[14,3,512]{2,1,0:T(4,128)}, f32[14,3,512]{2,1,0:T(4,128)}, u32[]{:S(2)}, u32[]{:S(2)}) collective-permute-start(f32[14,3,512]{2,1,0:T(4,128)} %get-tuple-element.63), channel_id=1, source_target_pairs={{0,1},{1,2},{2,3},{4,5},{5,6},{6,7},{8,9},{9,10},{10,11},{12,13},{... | collective-permute-start | bytes 258056 | tf_op jit(solution)/shard_map/ppermute | solution.py:33
  264.5 5.5 %collective-permute-start.5 = (f32[14,3,512]{2,1,0:T(4,128)S(1)}, f32[14,3,512]{2,1,0:T(4,128)S(1)}, u32[]{:S(2)}, u32[]{:S(2)}) collective-permute-start(f32[14,3,512]{2,1,0:T(4,128)S(1)} %get-tuple-element.62), channel_id=1, source_target_pairs={{1,0},{2,1},{3,2},{5,4},{6,5},{7,6},{9,8},{10,9},{11,10},{13,12},{... | collective-permute-start | bytes 258056 | tf_op jit(solution)/shard_map/ppermute | solution.py:33
  270.5 11.2 %copy-start.3 = (bf16[1,8,32,256]{3,2,1,0:T(8,128)(2,1)S(1)}, bf16[1,8,32,256]{3,2,1,0:T(8,128)(2,1)}, u32[]{:S(2)}) copy-start(bf16[1,8,32,256]{3,2,1,0:T(8,128)(2,1)} %param.19) | copy-start | bytes 393220
  270.5 11.2 %copy-start.15 = (f32[8,32]{1,0:T(8,128)S(1)}, f32[8,32]{1,0:T(8,128)}, u32[]{:S(2)}) copy-start(f32[8,32]{1,0:T(8,128)} %copy-done.14) | copy-start | bytes 3076
  270.5 11.2 %copy-start.20 = (f32[256]{0:T(256)S(1)}, f32[256]{0:T(256)}, u32[]{:S(2)}) copy-start(f32[256]{0:T(256)} %copy-done.19) | copy-start | bytes 3076
  270.5 4.1 %collective-permute-start.6 = (f32[3,32,512]{2,1,0:T(8,128)S(1)}, f32[3,32,512]{2,1,0:T(8,128)S(1)}, u32[]{:S(2)}, u32[]{:S(2)}) collective-permute-start(f32[3,32,512]{2,1,0:T(8,128)S(1)} %get-tuple-element.65), channel_id=1, source_target_pairs={{0,4},{4,8},{8,12},{1,5},{5,9},{9,13},{2,6},{6,10},{10,14},{3,7},{... | collective-permute-start | bytes 589832 | tf_op jit(solution)/shard_map/ppermute | solution.py:33
  272.0 9.5 %collective-permute-start.7 = (f32[3,32,512]{2,1,0:T(8,128)S(1)}, f32[3,32,512]{2,1,0:T(8,128)S(1)}, u32[]{:S(2)}, u32[]{:S(2)}) collective-permute-start(f32[3,32,512]{2,1,0:T(8,128)S(1)} %get-tuple-element.64), channel_id=1, source_target_pairs={{4,0},{8,4},{12,8},{5,1},{9,5},{13,9},{6,2},{10,6},{14,10},{7,3},{... | collective-permute-start | bytes 589832 | tf_op jit(solution)/shard_map/ppermute | solution.py:33
  281.6 1.0 copy-start.8
  282.6 1.2 copy-start.5
  282.6 108.4 %copy-start.13 = (f32[1024]{0:T(1024)S(1)}, f32[1024]{0:T(1024)}, u32[]{:S(2)}) copy-start(f32[1024]{0:T(1024)} %copy-done.12) | copy-start | bytes 12292
  282.6 109.3 %copy-start.18 = (f32[16]{0:T(128)S(1)}, f32[16]{0:T(128)}, u32[]{:S(2)}) copy-start(f32[16]{0:T(128)} %copy-done.17) | copy-start | bytes 196
Sparse Core Ops, SparseCore 0:
  102.5 103.7 reduce-scatter.1
where the time goes:
time: 401 us; the launch traced here: 400 us
  blocking collectives  316 us (79%)
  starting transfers between devices  18.3 us (5%)
  local copies, waits for them, and re-layouts  16.8 us (4%)
  between operations  15.5 us (4%)
  waiting for transfers between devices  13.7 us (3%)
  matrix products  10.7 us (3%)
  other arithmetic  8.66 us (2%)
    psum x1, blocking collectives, local(): lax.psum((coarse_qkv_local, coarse_out_local), 'batch')  131 us
    psum x1, blocking collectives, local(): lax.psum((grad_qkv_local, grad_out_local), ('batch', 'gy', 'gx'))  107 us
    all_gather x1, blocking collectives, local(): all_normed = lax.all_gather(coarse_normed, ('gy', 'gx'), axis=0, tiled=True)  44.2 us
    all_gather x1, blocking collectives, local(): all_cot = lax.all_gather(coarse_cot, ('gy', 'gx'), axis=0, tiled=True)  34 us
    ppermute x4, waiting for transfers between devices, shifted(): lax.ppermute(value, axis, [(source, source + steps) for source in range(l...  11 us
    ppermute x2, starting transfers between devices, padded_2(): before = lax.ppermute(last, axis, up)  8.95 us
  transfers between devices with their start and end apart: 9, of which 4 were waited for; matrix products, arithmetic and copies ran while one was open for 7% of the time, Pallas kernels for 0%

commit v1 on v0

--- a/solution.py
+++ b/solution.py
@@ -272,7 +272,10 @@
     coarse_shares = jnp.exp(coarse_scores - coarse_log)
     coarse_weights = coarse_shares.astype(jnp.bfloat16)
     head_mixed = contract("ts,se->te", coarse_weights, head_values).astype(jnp.bfloat16)
-    all_cot = lax.all_gather(coarse_cot, ("gy", "gx"), axis=0, tiled=True)
+    all_cot = jnp.concatenate(
+        lax.all_to_all(jnp.stack([coarse_cot] * lax.axis_size(("gy", "gx"))), ("gy", "gx"), 0, 0),
+        axis=0,
+    )
     head_upstream = contract("td,ed->te", all_cot, coarse_out).astype(jnp.bfloat16)
     coarse_out_local = contract("te,td->ed", head_mixed, all_cot)
     coarse_products = contract("te,se->ts", head_upstream, head_values)

time: 401 us -> 384 us (0.958)
  blocking collectives: 316 us -> 273 us
  starting transfers between devices: 18.3 us -> 32.6 us
  local copies, waits for them, and re-layouts: 16.8 us -> 24 us
    all_gather x1 -> x0, blocking collectives: 34 us -> none  [local(): all_cot = lax.all_gather(coarse_cot, ('gy', 'gx'), axis=0, tiled=True)]
    psum x1, blocking collectives: 131 us -> 114 us  [local(): lax.psum((coarse_qkv_local, coarse_out_local), 'batch')]
    all_to_all x0 -> x1, starting transfers between devices: none -> 13 us  [local(): lax.all_to_all(jnp.stack([coarse_cot] * lax.axis_size(('gy', 'gx'))), ('g...]
    psum x1, blocking collectives: 107 us -> 117 us  [local(): lax.psum((grad_qkv_local, grad_out_local), ('batch', 'gy', 'gx'))]
  transfers between devices with their start and end apart: 9 -> 10, of which waited for: 4 -> 4; matrix products, arithmetic and copies ran while one was open for 7% -> 9% of each run, Pallas kernels for 0% -> 0%
where the time goes in v1:
time: 384 us; the launch traced here: 379 us
  blocking collectives  273 us (71%)
  starting transfers between devices  32.6 us (8%)
  local copies, waits for them, and re-layouts  24 us (6%)
  between operations  15.5 us (4%)
  waiting for transfers between devices  12.4 us (3%)
  matrix products  11.8 us (3%)
  other arithmetic  10.2 us (3%)
    psum x1, blocking collectives, local(): lax.psum((grad_qkv_local, grad_out_local), ('batch', 'gy', 'gx'))  117 us
    psum x1, blocking collectives, local(): lax.psum((coarse_qkv_local, coarse_out_local), 'batch')  114 us
    all_gather x1, blocking collectives, local(): all_normed = lax.all_gather(coarse_normed, ('gy', 'gx'), axis=0, tiled=True)  41.1 us
    all_to_all x1, starting transfers between devices, local(): lax.all_to_all(jnp.stack([coarse_cot] * lax.axis_size(('gy', 'gx'))), ('g...  13 us
    ppermute x4, waiting for transfers between devices, shifted(): lax.ppermute(value, axis, [(source, source + steps) for source in range(l...  9.24 us
    ppermute x2, starting transfers between devices, padded_2(): before = lax.ppermute(last, axis, up)  8.99 us
    dot_general x16, matrix products, contract(): jnp.einsum(pattern, first_op, second_op, preferred_element_type=jnp.float32)  8.59 us
    ppermute x4, starting transfers between devices, shifted(): lax.ppermute(value, axis, [(source, source + steps) for source in range(l...  7.97 us
  transfers between devices with their start and end apart: 10, of which 4 were waited for; matrix products, arithmetic and copies ran while one was open for 9% of the time, Pallas kernels for 0%

profile of v1, /device:TPU:1, one launch (start us, length us, event | category | flops | bytes accessed | tf_op | source)
XLA Modules:
  0.0 379.4 jit_solution(3266631963050063219)
XLA Ops:
  7.9 1.0 fusion.28
  10.8 1.3 convolution_convert_fusion
  12.1 6.6 %collective-permute-start = (bf16[1,3,32,512]{3,2,1,0:T(8,128)(2,1)S(1)}, bf16[1,3,32,512]{3,2,1,0:T(8,128)(2,1)S(1)}, u32[]{:S(2)}, u32[]{:S(2)}) collective-permute-start(bf16[1,3,32,512]{3,2,1,0:T(8,128)(2,1)S(1)} %get-tuple-element.74), channel_id=1, source_target_pairs={{0,4},{4,8},{8,12},{1,5},{5,9},{9,13},{2,6},{6,10},{10,14},{3,7},{... | collective-permute-start | bytes 294920 | tf_op jit(solution)/shard_map/ppermute | solution.py:24
  18.7 1.3 collective-permute-start.1
  20.9 13.0 %all-to-all-start = ((bf16[16,16,1024]{2,1,0:T(8,128)(2,1)}), bf16[16,16,1024]{2,1,0:T(8,128)(2,1)S(1)}, u32[]{:S(2)}, u32[]{:S(2)}) async-start(bf16[16,16,1024]{2,1,0:T(8,128)(2,1)} %stack.15), calls=%async_computation | async-start | bytes 1048576 | tf_op jit(solution)/shard_map/all_to_all | solution.py:276
  34.8 41.1 %all_gather.3 = bf16[256,1024]{1,0:T(8,128)(2,1)S(1)} all-gather(bf16[16,1024]{1,0:T(8,128)(2,1)S(1)} %multiply_convert_fusion.2), channel_id=1, replica_groups=mesh['batch'=32,'gy'=4,'gx'=4] {'gy','gx'}, dimensions={0}, use_global_device_ids=true | all-gather | bytes 557056 | tf_op jit(solution)/shard_map/all_gather | solution.py:264
  77.9 2.4 collective-permute-start.2
  80.2 1.3 collective-permute-start.3
  82.3 3.1 collective-permute-done.3
  89.4 1.3 convolution_bitcast_fusion.1
  91.1 1.0 fusion.4
  92.2 1.3 convolution_bitcast_fusion.2
  94.5 2.0 copy.49
  96.6 2.0 concatenate.57
  98.6 2.0 copy.51
  100.6 1.9 concatenate.58
  102.5 1.4 constant_dynamic-update-slice_fusion.1
  105.0 1.0 copy.52
  106.8 2.3 collective-permute-start.4
  110.1 1.8 copy.46
  111.9 1.8 reshape_reshape.22
  113.8 1.3 collective-permute-start.5
  115.1 1.6 slice_add_fusion.3
  116.7 1.2 scatter-add.14
  117.9 1.7 collective-permute-done.5
  120.9 3.1 collective-permute-start.6
  124.2 1.3 collective-permute-start.7
  125.5 1.0 collective-permute-done.6
  126.5 6.5 %collective-permute-done.7 = f32[3,32,512]{2,1,0:T(8,128)S(1)} collective-permute-done((f32[3,32,512]{2,1,0:T(8,128)S(1)}, f32[3,32,512]{2,1,0:T(8,128)S(1)}, u32[]{:S(2)}, u32[]{:S(2)}) %collective-permute-start.7) | collective-permute-done | bytes 196640 | tf_op jit(solution)/shard_map/ppermute | solution.py:33
  135.3 117.5 %all-reduce.12 = (bf16[256,768]{1,0:T(8,128)(2,1)}, bf16[256,256]{1,0:T(8,128)(2,1)}) all-reduce(f32[256,768]{1,0:T(8,128)S(1)} %convolution_bitcast_fusion.3, f32[256,256]{1,0:T(8,128)S(1)} %copy-done.5), channel_id=1, replica_groups=mesh['batch'=32,'gy'=4,'gx'=4] {'batch','gy','gx'}, use_global_device_ids=true, to_apply=%region_11.12 | all-reduce | flops 262144 | bytes 1572864 | tf_op jit(solution)/shard_map/psum | solution.py:298
  253.9 1.1 fusion.1
  255.8 114.4 %all-reduce.11 = (bf16[3,64,1024]{2,1,0:T(8,128)(2,1)}, bf16[64,1024]{1,0:T(8,128)(2,1)}) all-reduce(f32[3,64,1024]{2,1,0:T(8,128)S(1)} %fusion.14, f32[64,1024]{1,0:T(8,128)S(1)} %fusion.9), channel_id=1, replica_groups=mesh['batch'=32,'gy'=4,'gx'=4] {'batch'}, use_global_device_ids=true, to_apply=%region_13.14 | all-reduce | flops 262144 | bytes 1572864 | tf_op jit(solution)/shard_map/psum | solution.py:299
  (132 shorter events, 22.1 us)
Async XLA Ops:
  7.2 69.6 %copy-start = (bf16[3,64,1024]{2,1,0:T(8,128)(2,1)S(1)}, bf16[3,64,1024]{2,1,0:T(8,128)(2,1)}, u32[]{:S(2)}) copy-start(bf16[3,64,1024]{2,1,0:T(8,128)(2,1)} %param.28) | copy-start | bytes 1179652
  7.2 12.9 %copy-start.16 = (bf16[1,4,4,1024]{3,2,1,0:T(4,128)(2,1)S(1)}, bf16[1,4,4,1024]{3,2,1,0:T(4,128)(2,1)}, u32[]{:S(2)}) copy-start(bf16[1,4,4,1024]{3,2,1,0:T(4,128)(2,1)} %param.22) | copy-start | bytes 98308
  10.8 23.3 %copy-start.14 = (bf16[1,4,4,1024]{3,2,1,0:T(4,128)(2,1)S(1)}, bf16[1,4,4,1024]{3,2,1,0:T(4,128)(2,1)}, u32[]{:S(2)}) copy-start(bf16[1,4,4,1024]{3,2,1,0:T(4,128)(2,1)} %param.21) | copy-start | bytes 98308
  12.0 22.2 %copy-start.17 = (f32[1024]{0:T(1024)S(1)}, f32[1024]{0:T(1024)}, u32[]{:S(2)}) copy-start(f32[1024]{0:T(1024)} %param.25) | copy-start | bytes 12292
  12.1 65.7 %collective-permute-start = (bf16[1,3,32,512]{3,2,1,0:T(8,128)(2,1)S(1)}, bf16[1,3,32,512]{3,2,1,0:T(8,128)(2,1)S(1)}, u32[]{:S(2)}, u32[]{:S(2)}) collective-permute-start(bf16[1,3,32,512]{3,2,1,0:T(8,128)(2,1)S(1)} %get-tuple-element.74), channel_id=1, source_target_pairs={{0,4},{4,8},{8,12},{1,5},{5,9},{9,13},{2,6},{6,10},{10,14},{3,7},{... | collective-permute-start | bytes 294920 | tf_op jit(solution)/shard_map/ppermute | solution.py:24
  18.7 59.1 %collective-permute-start.1 = (bf16[1,3,32,512]{3,2,1,0:T(8,128)(2,1)S(1)}, bf16[1,3,32,512]{3,2,1,0:T(8,128)(2,1)S(1)}, u32[]{:S(2)}, u32[]{:S(2)}) collective-permute-start(bf16[1,3,32,512]{3,2,1,0:T(8,128)(2,1)S(1)} %get-tuple-element.75), channel_id=1, source_target_pairs={{4,0},{8,4},{12,8},{5,1},{9,5},{13,9},{6,2},{10,6},{14,10},{7,3},{... | collective-permute-start | bytes 294920 | tf_op jit(solution)/shard_map/ppermute | solution.py:25
  20.9 56.5 %copy-start.9 = (bf16[1,8,32,256]{3,2,1,0:T(8,128)(2,1)S(1)}, bf16[1,8,32,256]{3,2,1,0:T(8,128)(2,1)}, u32[]{:S(2)}) copy-start(bf16[1,8,32,256]{3,2,1,0:T(8,128)(2,1)} %param.20) | copy-start | bytes 393220
  20.9 56.6 %copy-start.13 = (bf16[256,256]{1,0:T(8,128)(2,1)S(1)}, bf16[256,256]{1,0:T(8,128)(2,1)}, u32[]{:S(2)}) copy-start(bf16[256,256]{1,0:T(8,128)(2,1)} %param.27) | copy-start | bytes 393220
  20.9 231.8 %all-to-all-start = ((bf16[16,16,1024]{2,1,0:T(8,128)(2,1)}), bf16[16,16,1024]{2,1,0:T(8,128)(2,1)S(1)}, u32[]{:S(2)}, u32[]{:S(2)}) async-start(bf16[16,16,1024]{2,1,0:T(8,128)(2,1)} %stack.15), calls=%async_computation | async-start | bytes 1048576 | tf_op jit(solution)/shard_map/all_to_all | solution.py:276
  33.9 336.2 %reduce-scatter.2.cloned.1.call-start = ((), (), s32[]{:S(2)}) async-start(), calls=%async_computation.2 | async-start | bytes 557056 | tf_op jit(solution)/shard_map/reduce_scatter | solution.py:294
  75.9 0.8 copy-start.1
  77.1 4.9 %copy-start.6 = (bf16[3,256,64]{1,2,0:T(8,128)(2,1)}, bf16[3,256,64]{1,2,0:T(8,128)(2,1)S(1)}, u32[]{:S(2)}) copy-start(bf16[3,256,64]{1,2,0:T(8,128)(2,1)S(1)} %fusion.5) | copy-start | bytes 294916
  77.9 4.5 %collective-permute-start.2 = (bf16[1,14,3,512]{3,2,1,0:T(4,128)(2,1)S(1)}, bf16[1,14,3,512]{3,2,1,0:T(4,128)(2,1)S(1)}, u32[]{:S(2)}, u32[]{:S(2)}) collective-permute-start(bf16[1,14,3,512]{3,2,1,0:T(4,128)(2,1)S(1)} %get-tuple-element.72), channel_id=1, source_target_pairs={{0,1},{1,2},{2,3},{4,5},{5,6},{6,7},{8,9},{9,10},{10,11},{12,13},{... | collective-permute-start | bytes 129032 | tf_op jit(solution)/shard_map/ppermute | solution.py:24
  80.2 5.2 %collective-permute-start.3 = (bf16[1,14,3,512]{3,2,1,0:T(4,128)(2,1)S(1)}, bf16[1,14,3,512]{3,2,1,0:T(4,128)(2,1)S(1)}, u32[]{:S(2)}, u32[]{:S(2)}) collective-permute-start(bf16[1,14,3,512]{3,2,1,0:T(4,128)(2,1)S(1)} %get-tuple-element.73), channel_id=1, source_target_pairs={{1,0},{2,1},{3,2},{5,4},{6,5},{7,6},{9,8},{10,9},{11,10},{13,12},{... | collective-permute-start | bytes 129032 | tf_op jit(solution)/shard_map/ppermute | solution.py:25
  102.5 1.4 copy-start.3
  105.0 4.0 %copy-start.10 = (bf16[1,8,32,256]{3,2,1,0:T(8,128)(2,1)S(1)}, bf16[1,8,32,256]{3,2,1,0:T(8,128)(2,1)}, u32[]{:S(2)}) copy-start(bf16[1,8,32,256]{3,2,1,0:T(8,128)(2,1)} %param.20) | copy-start | bytes 393220
  105.0 4.0 %copy-start.11 = (bf16[1,8,4,8,256]{4,3,2,1,0:T(8,128)(2,1)S(1)}, bf16[1,8,4,8,256]{4,3,2,1,0:T(8,128)(2,1)}, u32[]{:S(2)}) copy-start(bf16[1,8,4,8,256]{4,3,2,1,0:T(8,128)(2,1)} %copy.54) | copy-start | bytes 393220
  106.8 8.3 %collective-permute-start.4 = (f32[14,3,512]{2,1,0:T(4,128)}, f32[14,3,512]{2,1,0:T(4,128)}, u32[]{:S(2)}, u32[]{:S(2)}) collective-permute-start(f32[14,3,512]{2,1,0:T(4,128)} %get-tuple-element.63), channel_id=1, source_target_pairs={{0,1},{1,2},{2,3},{4,5},{5,6},{6,7},{8,9},{9,10},{10,11},{12,13},{... | collective-permute-start | bytes 258056 | tf_op jit(solution)/shard_map/ppermute | solution.py:33
  113.8 5.8 %collective-permute-start.5 = (f32[14,3,512]{2,1,0:T(4,128)}, f32[14,3,512]{2,1,0:T(4,128)}, u32[]{:S(2)}, u32[]{:S(2)}) collective-permute-start(f32[14,3,512]{2,1,0:T(4,128)} %get-tuple-element.62), channel_id=1, source_target_pairs={{1,0},{2,1},{3,2},{5,4},{6,5},{7,6},{9,8},{10,9},{11,10},{13,12},{... | collective-permute-start | bytes 258056 | tf_op jit(solution)/shard_map/ppermute | solution.py:33
  116.7 7.4 %copy-start.8 = (bf16[1,4,8,8,256]{4,3,2,1,0:T(8,128)(2,1)S(1)}, bf16[1,4,8,8,256]{4,3,2,1,0:T(8,128)(2,1)}, u32[]{:S(2)}) copy-start(bf16[1,4,8,8,256]{4,3,2,1,0:T(8,128)(2,1)} %reshape_reshape.22) | copy-start | bytes 393220
  120.9 12.2 %copy-start.4 = (bf16[1,8,32,256]{3,2,1,0:T(8,128)(2,1)S(1)}, bf16[1,8,32,256]{3,2,1,0:T(8,128)(2,1)}, u32[]{:S(2)}) copy-start(bf16[1,8,32,256]{3,2,1,0:T(8,128)(2,1)} %param.19) | copy-start | bytes 393220
  120.9 5.6 %collective-permute-start.6 = (f32[3,32,512]{2,1,0:T(8,128)S(1)}, f32[3,32,512]{2,1,0:T(8,128)S(1)}, u32[]{:S(2)}, u32[]{:S(2)}) collective-permute-start(f32[3,32,512]{2,1,0:T(8,128)S(1)} %get-tuple-element.65), channel_id=1, source_target_pairs={{0,4},{4,8},{8,12},{1,5},{5,9},{9,13},{2,6},{6,10},{10,14},{3,7},{... | collective-permute-start | bytes 589832 | tf_op jit(solution)/shard_map/ppermute | solution.py:33
  124.2 8.9 %collective-permute-start.7 = (f32[3,32,512]{2,1,0:T(8,128)S(1)}, f32[3,32,512]{2,1,0:T(8,128)S(1)}, u32[]{:S(2)}, u32[]{:S(2)}) collective-permute-start(f32[3,32,512]{2,1,0:T(8,128)S(1)} %get-tuple-element.64), channel_id=1, source_target_pairs={{4,0},{8,4},{12,8},{5,1},{9,5},{13,9},{6,2},{10,6},{14,10},{7,3},{... | collective-permute-start | bytes 589832 | tf_op jit(solution)/shard_map/ppermute | solution.py:33
  133.1 1.0 copy-start.12
  134.1 1.2 copy-start.5
  134.1 118.7 %copy-start.15 = (bf16[64,1024]{1,0:T(8,128)(2,1)S(1)}, bf16[64,1024]{1,0:T(8,128)(2,1)}, u32[]{:S(2)}) copy-start(bf16[64,1024]{1,0:T(8,128)(2,1)} %param.29) | copy-start | bytes 393220
  134.5 118.8 %copy-start.7 = (bf16[3,256,64]{1,2,0:T(8,128)(2,1)S(1)}, bf16[3,256,64]{1,2,0:T(8,128)(2,1)}, u32[]{:S(2)}) copy-start(bf16[3,256,64]{1,2,0:T(8,128)(2,1)} %copy-done.6) | copy-start | bytes 294916
  253.6 1.9 copy-start.2
Sparse Core Ops, SparseCore 0:
  255.2 87.0 reduce-scatter.1
